TPU v7x, 32 devices: a whole 2x2x4 slice. The times are simulated.
32 devices in a mesh: vocab: 4 (over x, core), fsdp: 8 (over z, y).
Axes of the slice: x: 2, y: 2, z: 4, core: 2. Of those that a mesh axis runs over, the one named last changes fastest.
Arguments:
- hidden: bfloat16 [2, 384, 4096], P(None, 'fsdp'), may hold values from -1000 to 1000
- norm_gain: bfloat16 [4096], replicated, may hold values from 0.5 to 1.5
- labels: int32 [2, 384], P(None, 'fsdp'), may hold values from 0 to 65535
- head_weight: bfloat16 [4096, 65536], P(None, ('vocab', 'fsdp')), may hold values from -1 to 1
- head_ema: float32 [4096, 65536], P(None, ('vocab', 'fsdp')), may hold values from 1e-09 to 0.001
- gain_ema: float32 [4096], replicated, may hold values from 0.0001 to 0.03
Outputs:
- head_ema_new: float32 [4096, 65536], P(None, ('vocab', 'fsdp'))
- gain_ema_new: float32 [4096], replicated
All inputs are finite; a program needn't handle non-finite values.
Results may differ from a plain program's by a relative error of at most 0.00049.
Values may be sent and summed in bfloat16 or wider, within the bound.
A program may use at most 192 MiB of HBM per device.

v0:
```python
import jax
import jax.numpy as jnp
from jax import lax
from jax.sharding import PartitionSpec as P

BETA = 0.99
EPS = 1e-05


def on_device(hidden, norm_gain, labels, head_weight, head_ema, gain_ema):
    batches, own_rows, features = hidden.shape
    columns = head_weight.shape[1]
    column_ids = lax.iota(jnp.int32, columns)[None, :] + lax.axis_index(("vocab", "fsdp")) * columns
    gain_wide = norm_gain.astype(jnp.float32)
    wide = hidden.astype(jnp.float32)
    factor = lax.rsqrt(jnp.mean(wide * wide, axis=-1, keepdims=True) + EPS)
    scaled = (wide * factor * gain_wide).astype(jnp.bfloat16)
    count = batches * own_rows * lax.axis_size("fsdp")
    gradient = jnp.zeros((features, columns), jnp.float32)
    for batch in range(batches):
        batch_rows = scaled[batch]
        batch_labels = labels[batch]
        rows_all, labels_all = (
            lax.all_gather(batch_rows, "fsdp", axis=0, tiled=True),
            lax.all_gather(batch_labels, "fsdp", axis=0, tiled=True),
        )
        logits = jnp.dot(rows_all, head_weight, preferred_element_type=jnp.float32)
        local_top = jnp.max(logits, axis=1)
        row_top = lax.pmax(local_top, ("vocab", "fsdp"))
        local_total = jnp.sum(jnp.exp(logits - row_top[:, None]), axis=1)
        row_total = lax.psum(local_total, ("vocab", "fsdp"))
        chances = jnp.exp(logits - row_top[:, None]) / row_total[:, None]
        hits = (labels_all[:, None] == column_ids).astype(jnp.float32)
        slope = (chances - hits).astype(jnp.bfloat16)
        gradient = gradient + lax.dot_general(
            rows_all, slope, (((0,), (0,)), ((), ())), preferred_element_type=jnp.float32
        )
    head_new = BETA * head_ema + (1.0 - BETA) * gradient * gradient / count
    partial_sum = jnp.sum(head_weight.astype(jnp.float32) * gradient, axis=1)
    gain_grad = lax.psum(partial_sum, ("vocab", "fsdp")) / gain_wide
    gain_new = BETA * gain_ema + (1.0 - BETA) * gain_grad * gain_grad / count
    return (head_new, gain_new)


def solution(mesh):
    return jax.shard_map(
        on_device,
        mesh=mesh,
        in_specs=(
            P(None, "fsdp", None),
            P(),
            P(None, "fsdp"),
            P(None, ("vocab", "fsdp")),
            P(None, ("vocab", "fsdp")),
            P(),
        ),
        out_specs=(P(None, ("vocab", "fsdp")), P()),
        check_vma=False,
    )
```

profile of v0, /device:TPU:0, one launch (start us, length us, event | category | flops | bytes accessed | tf_op | source)
XLA Modules:
  0.0 369.3 jit_solution(13150943076576442699)
XLA Ops:
  7.2 0.0 all-gather.7.cloned.1.call-start
  7.2 1.4 fusion.11
  8.6 0.7 convert_element_type.25
  9.3 1.4 fusion.13
  10.7 0.9 fusion.24
  11.6 0.0 all-gather.7.cloned.1.call-update
  11.7 0.0 all-gather.9.cloned.1.call-start
  11.7 0.7 all-gather.9.cloned.1.call-update
  12.4 21.0 %copy.9 = bf16[4096,2048]{0,1:T(8,128)(2,1)} copy(bf16[4096,2048]{1,0:T(8,128)(2,1)} %param.9) | data formatting | bytes 33554432 | tf_op args[3]
  33.4 0.0 copy-start.3
  33.4 0.0 copy-start.2
  33.4 31.2 %copy.8 = f32[4096,2048]{0,1:T(8,128)} copy(f32[4096,2048]{1,0:T(8,128)} %param.10) | data formatting | bytes 67108864 | tf_op args[4]
  64.6 0.0 copy-done.3
  64.6 0.6 dynamic-slice
  65.8 0.0 copy-done.2
  65.9 0.1 bitcast_dynamic-update-slice_fusion.1
  66.0 0.1 bitcast_dynamic-update-slice_fusion
  66.0 13.1 %all-reduce.2 = (s32[384]{0:T(512)S(1)}, s32[384]{0:T(512)S(1)}) all-reduce(s32[384]{0:T(512)S(1)} %bitcast_dynamic-update-slice_fusion.1, s32[384]{0:T(512)S(1)} %bitcast_dynamic-update-slice_fusion), channel_id=3, replica_groups=mesh['vocab'=4,'fsdp'=8] {'fsdp'}, use_global_device_ids=true, to_apply=%add | all-reduce | flops 768 | bytes 6144
  79.1 0.0 all-gather.7.cloned.1.call-done
  79.1 11.5 %fusion.25 = (f32[384]{0:T(512)S(1)}, f32[384,2048]{1,0:T(8,128)S(1)}) fusion(bf16[4096,2048]{1,0:T(8,128)(2,1)} %param.9, bf16[1,384,4096]{2,1,0:T(8,128)(2,1)} %all-gather.7.cloned.1.call-done), kind=kOutput, calls=%fused_computation.39 | convolution fusion | flops 6443236864 | bytes 23070208 | tf_op jit(solution)/shard_map/dot_general | solution.py:27
  90.6 44.9 %all-gather.9.cloned.1.call-done = bf16[1,384,4096]{2,1,0:T(8,128)(2,1)} async-done(((bf16[1,48,4096]{2,1,0:T(8,128)(2,1)}), bf16[1,384,4096]{2,1,0:T(8,128)(2,1)}) %all-gather.9.cloned.1.call-update) | async-done | bytes 3145744 | tf_op jit(solution)/shard_map/all_gather | solution.py:24
  135.5 12.3 %fusion.26 = (f32[384]{0:T(512)S(1)}, f32[384,2048]{1,0:T(8,128)}) fusion(bf16[4096,2048]{1,0:T(8,128)(2,1)} %param.9, bf16[1,384,4096]{2,1,0:T(8,128)(2,1)} %all-gather.9.cloned.1.call-done), kind=kOutput, calls=%fused_computation.40 | convolution fusion | flops 6443236864 | bytes 23070208 | tf_op jit(solution)/shard_map/dot_general | solution.py:27
  147.8 39.2 %all-reduce.4 = (f32[384]{0:T(512)S(1)}, f32[384]{0:T(512)S(1)}) all-reduce(f32[384]{0:T(512)S(1)} %get-tuple-element.14, f32[384]{0:T(512)S(1)} %get-tuple-element.16), channel_id=1, replica_groups=mesh['vocab'=4,'fsdp'=8] {'vocab','fsdp'}, use_global_device_ids=true, to_apply=%region_2.0 | all-reduce | flops 768 | bytes 6144 | tf_op jit(solution)/shard_map/pmax | solution.py:29
  187.0 2.9 fusion.9
  189.9 40.1 %all-reduce.3 = (f32[384]{0:T(512)S(1)}, f32[384]{0:T(512)S(1)}) all-reduce(f32[384]{0:T(512)S(1)} %get-tuple-element.18, f32[384]{0:T(512)S(1)} %get-tuple-element.19), channel_id=1, replica_groups=mesh['vocab'=4,'fsdp'=8] {'vocab','fsdp'}, use_global_device_ids=true, to_apply=%region_4.0 | all-reduce | flops 768 | bytes 6144 | tf_op jit(solution)/shard_map/psum | solution.py:31
  229.9 17.4 %fusion.5 = f32[4096,2048]{0,1:T(8,128)} fusion(bf16[1,384,4096]{2,1,0:T(8,128)(2,1)} %all-gather.7.cloned.1.call-done, f32[384,2048]{1,0:T(8,128)S(1)} %get-tuple-element.15, s32[2048]{0:T(1024)S(1)} %iota_add_fusion, f32[384]{0:T(512)S(1)} %get-tuple-element.6, f32[384]{0:T(512)S(1)} %get-tuple-element.8, s32[384]{0:T(512)S(1)} %get-tuple-element.4), kind=kOutput, calls=%fused_computation.8 | convolution fusion | flops 6447169536 | bytes 39858688 | tf_op jit(solution)/shard_map/dot_general | solution.py:35
  247.3 41.1 %multiply_reduce_fusion = (f32[4096]{0:T(1024)S(1)}, f32[4096,2048]{0,1:T(8,128)}) fusion(bf16[4096,2048]{0,1:T(8,128)(2,1)} %copy.9, f32[4096,2048]{0,1:T(8,128)} %copy.8, f32[4096,2048]{0,1:T(8,128)} %fusion.5, f32[384,2048]{1,0:T(8,128)} %get-tuple-element.17, f32[384]{0:T(512)S(1)} %get-tuple-element.7, f32[384]{0:T(512)S(1)} %get-tuple-element.9, ...), kind=kOutput, calls=%fused_computation.3 | convolution fusion | flops 6522662912 | bytes 123761152 | tf_op jit(solution)/shard_map/dot_general | solution.py:35
  288.4 40.1 %psum.23 = f32[4096]{0:T(1024)S(1)} all-reduce(f32[4096]{0:T(1024)S(1)} %get-tuple-element.10), channel_id=1, replica_groups=mesh['vocab'=4,'fsdp'=8] {'vocab','fsdp'}, use_global_device_ids=true, to_apply=%region_10.0 | all-reduce | flops 4096 | bytes 32768 | tf_op jit(solution)/shard_map/psum | solution.py:40
  328.5 0.0 copy-start
  328.5 0.0 copy-start.1
  328.5 33.4 %copy.10 = f32[4096,2048]{1,0:T(8,128)} copy(f32[4096,2048]{0,1:T(8,128)} %get-tuple-element.11) | data formatting | bytes 67108864
  361.9 0.0 copy-done
  361.9 0.0 copy-done.1
  361.9 0.6 fusion.23
  (4 shorter events, 0.0 us)
Async XLA Ops:
  7.2 72.0 %all-gather.7.cloned.1.call-start = ((), (), s32[]{:S(2)}) async-start(), calls=%async_computation | async-start | bytes 3538944 | tf_op jit(solution)/shard_map/all_gather | solution.py:24
  11.7 123.8 %all-gather.9.cloned.1.call-start = ((), (), s32[]{:S(2)}) async-start(), calls=%async_computation.1 | async-start | bytes 3538944 | tf_op jit(solution)/shard_map/all_gather | solution.py:24
  33.4 31.2 %copy-start.3 = (u32[32]{0:T(128)S(1)}, u32[32]{0:T(128)}, u32[]{:S(2)}) copy-start(u32[32]{0:T(128)} %constant.34) | copy-start | bytes 388
  33.4 32.4 %copy-start.2 = (s32[2,48]{1,0:T(2,128)S(1)}, s32[2,48]{1,0:T(2,128)}, u32[]{:S(2)}) copy-start(s32[2,48]{1,0:T(2,128)} %param.8) | copy-start | bytes 1156
  328.5 33.4 %copy-start = (bf16[4096]{0:T(1024)(128)(2,1)S(1)}, bf16[4096]{0:T(1024)(128)(2,1)}, u32[]{:S(2)}) copy-start(bf16[4096]{0:T(1024)(128)(2,1)} %param.7) | copy-start | bytes 24580
  328.5 33.4 %copy-start.1 = (f32[4096]{0:T(1024)S(1)}, f32[4096]{0:T(1024)}, u32[]{:S(2)}) copy-start(f32[4096]{0:T(1024)} %param.11) | copy-start | bytes 49156
Sparse Core Ops, SparseCore 0:
  11.8 62.7 all-gather.6
  76.7 58.7 all-gather.8
where the time goes:
time: 371 us; the launch traced here: 369 us
  blocking collectives  132 us (36%)
  local copies, waits for them, and re-layouts  87.3 us (24%)
  matrix products  82.3 us (22%)
  waiting for transfers between devices  45.6 us (12%)
  between operations  14.7 us (4%)
  other arithmetic  6.97 us (2%)
    unnamed x16, local copies, waits for them, and re-layouts  86.3 us
    dot_general x2, matrix products, on_device(): lax.dot_general(rows_all, slope, (((0,), (0,)), ((), ())), preferred_elem...  58.5 us
    all_gather x2, waiting for transfers between devices, on_device(): lax.all_gather(batch_rows, 'fsdp', axis=0, tiled=True)  44.9 us
    psum x1, blocking collectives, on_device(): row_total = lax.psum(local_total, ('vocab', 'fsdp'))  40.1 us
    psum x1, blocking collectives, on_device(): gain_grad = lax.psum(partial_sum, ('vocab', 'fsdp')) / gain_wide  40.1 us
    pmax x1, blocking collectives, on_device(): row_top = lax.pmax(local_top, ('vocab', 'fsdp'))  39.2 us
    dot_general x2, matrix products, on_device(): logits = jnp.dot(rows_all, head_weight, preferred_element_type=jnp.float32)  23.8 us
    unnamed x1, blocking collectives  13.1 us
  transfers between devices with their start and end apart: 2, of which 1 were waited for; matrix products, arithmetic and copies ran while one was open for 17% of the time, Pallas kernels for 0%

commit v1 on v0

v1 whole, which is shorter than its diff:
```python
import functools

import jax
import jax.numpy as jnp
from jax import lax
from jax.experimental import pallas as pl
from jax.experimental.pallas import tpu as pltpu
from jax.sharding import PartitionSpec as P

BETA = 0.99
EPS = 1e-05
LANES = 128
MESH = pl.DeviceIdType.MESH
VMEM_LIMIT = 60 * 1024 * 1024


def bits_of(size):
    return [1 << place for place in reversed(range(size.bit_length() - 1))]


def flip(index, mask):
    for place in range(mask.bit_length()):
        bit = 1 << place
        if mask & bit:
            index = index + bit - 2 * bit * lax.rem(lax.div(index, bit), 2)
    return index


def shared_width(features, ways):
    return features // 8 // LANES * LANES if ways == 4 else 0


def gather_sends(parts, ways, features):
    return (parts - 1) * (ways + (2 if shared_width(features, ways) else 0))


def gather_kernel(parts, ways, own_ref, all_ref, send_sem, recv_sem, local_sem):
    part, way = lax.axis_index("fsdp"), lax.axis_index("vocab")
    features = own_ref.shape[1]
    both = shared_width(features, ways)
    single = (features - 2 * both) // ways
    part_bits, way_bits = bits_of(parts), bits_of(ways)

    barrier = pltpu.get_barrier_semaphore()
    for bit in part_bits:
        pl.semaphore_signal(barrier, inc=1, device_id=(way, flip(part, bit)), device_id_type=MESH)
    for bit in way_bits:
        pl.semaphore_signal(barrier, inc=1, device_id=(flip(way, bit), part), device_id_type=MESH)
    pl.semaphore_wait(barrier, len(part_bits) + len(way_bits))

    kinds = ([("both", [1])] if both else []) + [("single", way_bits)]

    def columns(kind, piece_mask):
        piece = flip(way, piece_mask)
        if kind == "both":
            return pl.ds(pl.multiple_of(single * ways + lax.rem(piece, 2) * both, LANES), both)
        return pl.ds(pl.multiple_of(piece * single, LANES), single)

    def slot(kind, part_mask, piece_mask):
        return (part_mask - 1) * (ways + 2) + (ways if kind == "both" else 0) + piece_mask

    sends = []

    def send(kind, part_mask, piece_mask, part_bit, way_bit):
        where = columns(kind, piece_mask)
        shard = flip(part, part_mask)
        target = all_ref.at[shard, :, where]
        copy = pltpu.make_async_remote_copy(
            src_ref=target if part_mask else own_ref.at[:, where],
            dst_ref=target,
            send_sem=send_sem.at[len(sends)],
            recv_sem=recv_sem.at[slot(kind, part_mask ^ part_bit, piece_mask ^ way_bit)],
            device_id=(flip(way, way_bit), flip(part, part_bit)),
            device_id_type=MESH,
        )
        copy.start()
        sends.append(copy)

    def forward(kind, kind_bits, part_mask, piece_mask):
        if not piece_mask:
            for bit in part_bits:
                if not part_mask or bit < part_mask & -part_mask:
                    send(kind, part_mask, 0, bit, 0)
        if part_mask:
            for bit in kind_bits:
                if not piece_mask or bit < piece_mask & -piece_mask:
                    send(kind, part_mask, piece_mask, 0, bit)

    def arrive(kind, part_mask, piece_mask):
        target = all_ref.at[flip(part, part_mask), :, columns(kind, piece_mask)]
        pltpu.make_async_remote_copy(
            src_ref=target,
            dst_ref=target,
            send_sem=send_sem.at[0],
            recv_sem=recv_sem.at[slot(kind, part_mask, piece_mask)],
            device_id=(flip(way, way_bits[-1]), part),
            device_id_type=MESH,
        ).wait_recv()

    keep = pltpu.make_async_copy(own_ref, all_ref.at[part], local_sem)
    for kind, kind_bits in reversed(kinds):
        forward(kind, kind_bits, 0, 0)
    keep.start()
    order = sorted(range(1, parts), key=lambda mask: (mask.bit_count(), -mask))
    for part_mask in order:
        for kind, kind_bits in reversed(kinds):
            arrive(kind, part_mask, 0)
            forward(kind, kind_bits, part_mask, 0)
    for last in (False, True):
        for part_mask in order:
            for kind, kind_bits in reversed(kinds):
                for piece_mask in range(1, 2 * kind_bits[0]):
                    if (piece_mask % 2 == 1) == last:
                        arrive(kind, part_mask, piece_mask)
                        forward(kind, kind_bits, part_mask, piece_mask)
    for copy in sends:
        copy.wait_send()
    keep.wait()


def gather_rows(own, parts, ways):
    rows, features = own.shape
    sends = gather_sends(parts, ways, features)
    return pl.pallas_call(
        functools.partial(gather_kernel, parts, ways),
        out_shape=jax.ShapeDtypeStruct((parts, rows, features), own.dtype),
        in_specs=[pl.BlockSpec(memory_space=pltpu.VMEM)],
        out_specs=pl.BlockSpec(memory_space=pl.ANY),
        scratch_shapes=[
            pltpu.SemaphoreType.DMA((sends,)),
            pltpu.SemaphoreType.DMA(((parts - 1) * (ways + 2),)),
            pltpu.SemaphoreType.DMA,
        ],
        compiler_params=pltpu.CompilerParams(collective_id=0, has_side_effects=True),
        name="gather_rows",
    )(own)


def exchange_kernel(parts, ways, combine, x_ref, y_ref, part_slots, way_slots, half, send_sem, part_sem, way_sem):
    part, way = lax.axis_index("fsdp"), lax.axis_index("vocab")
    barrier = pltpu.get_barrier_semaphore()
    for step in range(1, parts):
        pl.semaphore_signal(barrier, inc=1, device_id=(way, lax.rem(part + step, parts)), device_id_type=MESH)
    for step in range(1, ways):
        pl.semaphore_signal(barrier, inc=1, device_id=(lax.rem(way + step, ways), part), device_id_type=MESH)
    pl.semaphore_wait(barrier, parts + ways - 2)

    copies = []
    for step in range(1, parts):
        copies.append(
            pltpu.make_async_remote_copy(
                src_ref=x_ref,
                dst_ref=part_slots.at[part],
                send_sem=send_sem.at[step - 1],
                recv_sem=part_sem.at[step - 1],
                device_id=(way, lax.rem(part + step, parts)),
                device_id_type=MESH,
            )
        )
        copies[-1].start()
    part_slots[part] = x_ref[...]
    for step in range(1, parts):
        pltpu.make_async_remote_copy(
            src_ref=x_ref,
            dst_ref=part_slots.at[lax.rem(part + parts - step, parts)],
            send_sem=send_sem.at[step - 1],
            recv_sem=part_sem.at[step - 1],
            device_id=(way, lax.rem(part + step, parts)),
            device_id_type=MESH,
        ).wait_recv()
    half[...] = combine([part_slots[index] for index in range(parts)], False)
    for step in range(1, ways):
        copies.append(
            pltpu.make_async_remote_copy(
                src_ref=half,
                dst_ref=way_slots.at[way],
                send_sem=send_sem.at[parts - 2 + step],
                recv_sem=way_sem.at[step - 1],
                device_id=(lax.rem(way + step, ways), part),
                device_id_type=MESH,
            )
        )
        copies[-1].start()
    way_slots[way] = half[...]
    for step in range(1, ways):
        pltpu.make_async_remote_copy(
            src_ref=half,
            dst_ref=way_slots.at[lax.rem(way + ways - step, ways)],
            send_sem=send_sem.at[parts - 2 + step],
            recv_sem=way_sem.at[step - 1],
            device_id=(lax.rem(way + step, ways), part),
            device_id_type=MESH,
        ).wait_recv()
    y_ref[...] = combine([way_slots[index] for index in range(ways)], True)
    for copy in copies:
        copy.wait_send()


def exchange(x, parts, ways, combine, number, name):
    return pl.pallas_call(
        functools.partial(exchange_kernel, parts, ways, combine),
        out_shape=jax.ShapeDtypeStruct(x.shape, x.dtype),
        in_specs=[pl.BlockSpec(memory_space=pltpu.VMEM)],
        out_specs=pl.BlockSpec(memory_space=pltpu.VMEM),
        scratch_shapes=[
            pltpu.VMEM((parts,) + x.shape, x.dtype),
            pltpu.VMEM((ways,) + x.shape, x.dtype),
            pltpu.VMEM(x.shape, x.dtype),
            pltpu.SemaphoreType.DMA((parts + ways - 2,)),
            pltpu.SemaphoreType.DMA((parts - 1,)),
            pltpu.SemaphoreType.DMA((ways - 1,)),
        ],
        compiler_params=pltpu.CompilerParams(collective_id=number, has_side_effects=True),
        name=name,
    )(x)


def combine_stats(terms, labels_done):
    top = functools.reduce(jnp.maximum, [term[0:1] for term in terms])
    total = sum(term[1:2] * jnp.exp(term[0:1] - top) for term in terms)
    label = terms[0][2:3] if labels_done else sum(term[2:3] for term in terms)
    return jnp.concatenate([top, total, label, jnp.zeros((5, top.shape[1]), jnp.float32)], axis=0)


def combine_sum(terms, labels_done):
    return sum(terms)


def logits_kernel(rows_ref, weight_ref, label_ref, logits_ref, stats_ref, top_ref, total_ref):
    step = pl.program_id(0)

    @pl.when(step == 0)
    def _():
        top_ref[...] = jnp.full_like(top_ref, -jnp.inf)
        total_ref[...] = jnp.zeros_like(total_ref)

    logits_ref[...] = jnp.dot(rows_ref[...], weight_ref[...], preferred_element_type=jnp.float32)
    groups = [logits_ref[:, start : start + LANES] for start in range(0, logits_ref.shape[1], LANES)]
    old = top_ref[...]
    top = functools.reduce(jnp.maximum, groups, old)
    total_ref[...] = total_ref[...] * jnp.exp(old - top) + sum(jnp.exp(group - top) for group in groups)
    top_ref[...] = top

    @pl.when(step == pl.num_programs(0) - 1)
    def _():
        wide_top = top_ref[...].T
        row_top = jnp.max(wide_top, axis=0, keepdims=True)
        row_total = jnp.sum(total_ref[...].T * jnp.exp(wide_top - row_top), axis=0, keepdims=True)
        stats_ref[...] = jnp.concatenate(
            [row_top, row_total, label_ref[...], jnp.zeros((5, row_top.shape[1]), jnp.float32)], axis=0
        )


def local_logits(rows_all, head_weight, label_row):
    rows, features = rows_all.shape
    columns = head_weight.shape[1]
    tile = min(256, columns)
    return pl.pallas_call(
        logits_kernel,
        grid=(columns // tile,),
        out_shape=(
            jax.ShapeDtypeStruct((rows, columns), jnp.float32),
            jax.ShapeDtypeStruct((8, rows), jnp.float32),
        ),
        in_specs=[
            pl.BlockSpec((rows, features), lambda i: (0, 0), pipeline_mode=pl.Buffered(1)),
            pl.BlockSpec((features, tile), lambda i: (0, i)),
            pl.BlockSpec((1, rows), lambda i: (0, 0)),
        ],
        out_specs=(pl.BlockSpec((rows, tile), lambda i: (0, i)), pl.BlockSpec((8, rows), lambda i: (0, 0))),
        scratch_shapes=[pltpu.VMEM((rows, LANES), jnp.float32)] * 2,
        compiler_params=pltpu.CompilerParams(vmem_limit_bytes=VMEM_LIMIT),
        name="local_logits",
    )(rows_all, head_weight, label_row)


def update_kernel(
    chunk, rows_ref, stats_ref, logits_ref, weight_ref, ema_ref, new_ref, gain_ref, slope_ref, top_ref, scale_ref, label_ref
):
    count, columns = logits_ref.shape

    @pl.when(pl.program_id(0) == 0)
    def _():
        stats = stats_ref[...]
        top_ref[...] = jnp.broadcast_to(stats[0:1], (LANES, count)).T
        scale_ref[...] = jnp.broadcast_to(1.0 / stats[1:2], (LANES, count)).T
        label_ref[...] = jnp.broadcast_to(stats[2:3], (LANES, count)).T
        first = (lax.axis_index("vocab") * lax.axis_size("fsdp") + lax.axis_index("fsdp")) * columns

        @pl.loop(0, count // chunk)
        def _(index):
            some = pl.ds(pl.multiple_of(index * chunk, chunk), chunk)
            top, scale, label = top_ref[some, :], scale_ref[some, :], label_ref[some, :].astype(jnp.int32)
            label = label - first
            lane = lax.broadcasted_iota(jnp.int32, (chunk, LANES), 1)
            for start in range(0, columns, LANES):
                chances = jnp.exp(logits_ref[some, start : start + LANES] - top) * scale
                hits = (label == lane + start).astype(jnp.float32)
                slope_ref[some, start : start + LANES] = (chances - hits).astype(slope_ref.dtype)

    mix = (1.0 - BETA) / count
    tall = rows_ref[...].T
    total = jnp.zeros((tall.shape[0], LANES), jnp.float32)
    width = min(512, columns)
    for start in range(0, columns, width):
        gradient = jnp.dot(tall, slope_ref[:, start : start + width], preferred_element_type=jnp.float32)
        new_ref[:, start : start + width] = BETA * ema_ref[:, start : start + width] + mix * gradient * gradient
        product = weight_ref[:, start : start + width].astype(jnp.float32) * gradient
        for lane in range(0, width, LANES):
            total = total + product[:, lane : lane + LANES]
    gain_ref[...] = jnp.sum(total.T, axis=0, keepdims=True)


def head_update(rows_all, stats, logits, head_weight, head_ema, chunk):
    rows, features = rows_all.shape
    columns = head_weight.shape[1]
    tile = 256
    once = dict(pipeline_mode=pl.Buffered(1))
    return pl.pallas_call(
        functools.partial(update_kernel, chunk),
        grid=(features // tile,),
        out_shape=(
            jax.ShapeDtypeStruct((features, columns), jnp.float32),
            jax.ShapeDtypeStruct((1, features), jnp.float32),
        ),
        in_specs=[
            pl.BlockSpec((rows, tile), lambda i: (0, i)),
            pl.BlockSpec((8, rows), lambda i: (0, 0)),
            pl.BlockSpec((rows, columns), lambda i: (0, 0), **once),
            pl.BlockSpec((tile, columns), lambda i: (i, 0)),
            pl.BlockSpec((tile, columns), lambda i: (i, 0)),
        ],
        out_specs=(pl.BlockSpec((tile, columns), lambda i: (i, 0)), pl.BlockSpec((1, tile), lambda i: (0, i))),
        scratch_shapes=[pltpu.VMEM((rows, columns), jnp.bfloat16)] + [pltpu.VMEM((rows, LANES), jnp.float32)] * 3,
        compiler_params=pltpu.CompilerParams(vmem_limit_bytes=VMEM_LIMIT),
        name="head_update",
    )(rows_all, stats, logits, head_weight, head_ema)


def on_device(parts, ways, hidden, norm_gain, labels, head_weight, head_ema, gain_ema):
    batches, own_rows, features = hidden.shape
    own = batches * own_rows
    count = own * parts
    gain_wide = norm_gain.astype(jnp.float32)
    wide = hidden.reshape(own, features).astype(jnp.float32)
    factor = lax.rsqrt(jnp.mean(wide * wide, axis=-1, keepdims=True) + EPS)
    scaled = (wide * factor * gain_wide).astype(jnp.bfloat16)
    mine = lax.iota(jnp.int32, parts)[:, None] == lax.axis_index("fsdp")
    label_row = jnp.where(mine, labels.reshape(1, own).astype(jnp.float32), 0.0).reshape(1, count)

    rows_all = gather_rows(scaled, parts, ways).reshape(count, features)
    logits, stats = local_logits(rows_all, head_weight, label_row)
    stats = exchange(stats, parts, ways, combine_stats, 1, "exchange_stats")
    head_new, partial_sum = head_update(rows_all, stats, logits, head_weight, head_ema, own)
    gain_grad = exchange(partial_sum, parts, ways, combine_sum, 2, "exchange_gain").reshape(features) / gain_wide
    gain_new = BETA * gain_ema + (1.0 - BETA) * gain_grad * gain_grad / count
    return (head_new, gain_new)


def solution(mesh):
    return jax.shard_map(
        functools.partial(on_device, mesh.shape["fsdp"], mesh.shape["vocab"]),
        mesh=mesh,
        in_specs=(
            P(None, "fsdp", None),
            P(),
            P(None, "fsdp"),
            P(None, ("vocab", "fsdp")),
            P(None, ("vocab", "fsdp")),
            P(),
        ),
        out_specs=(P(None, ("vocab", "fsdp")), P()),
        check_vma=False,
    )
```

time: 371 us -> 138 us (0.37)
  blocking collectives: 132 us -> 0 us
  Pallas kernels: 0 us -> 130 us
  local copies, waits for them, and re-layouts: 87.3 us -> 0.84 us
  matrix products: 82.3 us -> 0 us
  waiting for transfers between devices: 45.6 us -> 0 us
  between operations: 14.7 us -> 0.7 us
    pallas_call x0 -> x5, Pallas kernels: none -> 130 us  [the longest x1 44 us: head_update(): pl.pallas_call(functools.partial(update_kernel, chunk), grid=(features //...]
    unnamed x16 -> x4, local copies, waits for them, and re-layouts: 86.3 us -> 0.01 us
    dot_general x4 -> x0, matrix products: 82.3 us -> none  [the longest x2 58.5 us: on_device(): lax.dot_general(rows_all, slope, (((0,), (0,)), ((), ())), preferred_elem...]
    psum x2 -> x0, blocking collectives: 80.1 us -> none  [the longest x1 40.1 us: on_device(): row_total = lax.psum(local_total, ('vocab', 'fsdp'))]
    all_gather x2 -> x0, waiting for transfers between devices: 44.9 us -> none  [on_device(): lax.all_gather(batch_rows, 'fsdp', axis=0, tiled=True)]
    pmax x1 -> x0, blocking collectives: 39.2 us -> none  [on_device(): row_top = lax.pmax(local_top, ('vocab', 'fsdp'))]
    unnamed x1 -> x0, blocking collectives: 13.1 us -> none
  transfers between devices with their start and end apart: 2 -> 0, of which waited for: 1 -> 0; matrix products, arithmetic and copies ran while one was open for 17% -> 0% of each run, Pallas kernels for 0% -> 0%
where the time goes in v1:
time: 138 us
  Pallas kernels  130 us (94%)
  other arithmetic  6.46 us (5%)
    pallas_call x1, Pallas kernels, head_update(): pl.pallas_call(functools.partial(update_kernel, chunk), grid=(features //...  44 us
    pallas_call x1, Pallas kernels, gather_rows(): pl.pallas_call(functools.partial(gather_kernel, parts, ways), out_shape=j...  41.2 us
    pallas_call x2, Pallas kernels, exchange(): pl.pallas_call(functools.partial(exchange_kernel, parts, ways, combine),...  24.8 us
    pallas_call x1, Pallas kernels, local_logits(): pl.pallas_call(logits_kernel, grid=(columns // tile,), out_shape=(jax.Sha...  19.6 us

profile of v1, /device:TPU:0, one launch (start us, length us, event | category | flops | bytes accessed | tf_op | source)
XLA Modules:
  0.0 137.6 jit_solution(1382479354233857203)
XLA Ops:
  0.6 0.7 convert_element_type.31
  1.3 0.1 convert_element_type.32
  1.4 1.4 %multiply_reduce_fusion = f32[2,48]{1,0:T(2,128)S(1)} fusion(bf16[2,48,4096]{2,1,0:T(8,128)(2,1)} %param.6), kind=kLoop, calls=%fused_computation.3 | loop fusion | flops 1179552 | bytes 786816 | tf_op jit(solution)/shard_map/reduce_sum | solution.py:346
  2.8 0.1 rsqrt.12
  2.9 0.1 broadcast_select_fusion
  3.0 0.7 select_n.15.label_ref
  3.6 0.7 convert_element_type.29
  4.3 2.3 %fusion.1.own_ref = bf16[96,4096]{1,0:T(8,128)(2,1)} fusion(f32[4096]{0:T(1024)S(1)} %convert_element_type.29, f32[96]{0:T(128)S(1)} %rsqrt.12, bf16[2,48,4096]{2,1,0:T(8,128)(2,1)} %param.6), kind=kLoop, calls=%fused_computation.2 | loop fusion | flops 1572864 | bytes 1589632 | tf_op jit(solution)/shard_map/convert_element_type | solution.py:347
  6.6 41.2 %gather_rows.1 = bf16[8,96,4096]{2,1,0:T(8,128)(2,1)} custom-call(bf16[96,4096]{1,0:T(8,128)(2,1)} %fusion.1.own_ref), custom_call_target="tpu_custom_call" | custom-call | tf_op jit(solution)/shard_map/gather_rows/pallas_call | solution.py:124
  47.8 19.6 %local_logits.1 = (f32[768,2048]{1,0:T(8,128)}, f32[8,768]{1,0:T(8,128)}) custom-call(bf16[768,4096]{1,0:T(8,128)(2,1)} %bitcast.8, bf16[4096,2048]{1,0:T(8,128)(2,1)} %weight_ref.3, f32[1,768]{1,0:T(1,128)} %select_n.15.label_ref), custom_call_target="tpu_custom_call" | custom-call | tf_op jit(solution)/shard_map/local_logits/pallas_call | solution.py:258
  67.4 12.0 %exchange_stats.1.stats_ref = f32[8,768]{1,0:T(8,128)} custom-call(f32[8,768]{1,0:T(8,128)} %get-tuple-element.6.x_ref), custom_call_target="tpu_custom_call" | custom-call | tf_op jit(solution)/shard_map/exchange_stats/pallas_call | solution.py:200
  79.4 0.0 copy-start
  79.4 0.0 copy-start.1
  79.4 44.0 %head_update.1 = (f32[4096,2048]{1,0:T(8,128)}, f32[1,4096]{1,0:T(1,128)}) custom-call(bf16[768,4096]{1,0:T(8,128)(2,1)} %bitcast.9, f32[8,768]{1,0:T(8,128)} %exchange_stats.1.stats_ref, f32[768,2048]{1,0:T(8,128)} %get-tuple-element.7.logits_ref, bf16[4096,2048]{1,0:T(8,128)(2,1)} %weight_ref.3, f32[4096,2048]{1,0:T(8,128)} %ema_ref.1), custom_call_target="tpu_custom_call" | custom-call | tf_op jit(solution)/shard_map/head_update/pallas_call | solution.py:319
  123.5 12.7 %exchange_gain.1 = f32[1,4096]{1,0:T(1,128)} custom-call(f32[1,4096]{1,0:T(1,128)} %get-tuple-element.9.x_ref), custom_call_target="tpu_custom_call" | custom-call | tf_op jit(solution)/shard_map/exchange_gain/pallas_call | solution.py:200
  136.2 0.0 copy-done
  136.3 0.0 copy-done.1
  136.3 1.3 fusion.3
  (2 shorter events, 0.0 us)
Async XLA Ops:
  79.4 56.8 %copy-start = (bf16[4096]{0:T(1024)(128)(2,1)S(1)}, bf16[4096]{0:T(1024)(128)(2,1)}, u32[]{:S(2)}) copy-start(bf16[4096]{0:T(1024)(128)(2,1)} %param.7) | copy-start | bytes 24580
  79.4 56.8 %copy-start.1 = (f32[4096]{0:T(1024)S(1)}, f32[4096]{0:T(1024)}, u32[]{:S(2)}) copy-start(f32[4096]{0:T(1024)} %param.11) | copy-start | bytes 49156

commit v2 on v1

--- a/solution.py
+++ b/solution.py
@@ -12,6 +12,12 @@
 LANES = 128
 MESH = pl.DeviceIdType.MESH
 VMEM_LIMIT = 60 * 1024 * 1024
+
+
+def normalize_kernel(hidden_ref, gain_ref, scaled_ref):
+    wide = hidden_ref[...].astype(jnp.float32)
+    factor = lax.rsqrt(jnp.mean(wide * wide, axis=-1, keepdims=True) + EPS)
+    scaled_ref[...] = (wide * factor * gain_ref[...].astype(jnp.float32)).astype(jnp.bfloat16)
 
 
 def bits_of(size):
@@ -219,7 +225,7 @@
     top = functools.reduce(jnp.maximum, [term[0:1] for term in terms])
     total = sum(term[1:2] * jnp.exp(term[0:1] - top) for term in terms)
     label = terms[0][2:3] if labels_done else sum(term[2:3] for term in terms)
-    return jnp.concatenate([top, total, label, jnp.zeros((5, top.shape[1]), jnp.float32)], axis=0)
+    return jnp.concatenate([top, total, label, jnp.zeros((1, top.shape[1]), jnp.float32)], axis=0)
 
 
 def combine_sum(terms, labels_done):
@@ -247,7 +253,7 @@
         row_top = jnp.max(wide_top, axis=0, keepdims=True)
         row_total = jnp.sum(total_ref[...].T * jnp.exp(wide_top - row_top), axis=0, keepdims=True)
         stats_ref[...] = jnp.concatenate(
-            [row_top, row_total, label_ref[...], jnp.zeros((5, row_top.shape[1]), jnp.float32)], axis=0
+            [row_top, row_total, label_ref[...], jnp.zeros((1, row_top.shape[1]), jnp.float32)], axis=0
         )
 
 
@@ -260,14 +266,14 @@
         grid=(columns // tile,),
         out_shape=(
             jax.ShapeDtypeStruct((rows, columns), jnp.float32),
-            jax.ShapeDtypeStruct((8, rows), jnp.float32),
+            jax.ShapeDtypeStruct((4, rows), jnp.float32),
         ),
         in_specs=[
             pl.BlockSpec((rows, features), lambda i: (0, 0), pipeline_mode=pl.Buffered(1)),
             pl.BlockSpec((features, tile), lambda i: (0, i)),
             pl.BlockSpec((1, rows), lambda i: (0, 0)),
         ],
-        out_specs=(pl.BlockSpec((rows, tile), lambda i: (0, i)), pl.BlockSpec((8, rows), lambda i: (0, 0))),
+        out_specs=(pl.BlockSpec((rows, tile), lambda i: (0, i)), pl.BlockSpec((4, rows), lambda i: (0, 0))),
         scratch_shapes=[pltpu.VMEM((rows, LANES), jnp.float32)] * 2,
         compiler_params=pltpu.CompilerParams(vmem_limit_bytes=VMEM_LIMIT),
         name="local_logits",
@@ -314,7 +320,7 @@
 def head_update(rows_all, stats, logits, head_weight, head_ema, chunk):
     rows, features = rows_all.shape
     columns = head_weight.shape[1]
-    tile = 256
+    tile = 512 if features % 512 == 0 else 256
     once = dict(pipeline_mode=pl.Buffered(1))
     return pl.pallas_call(
         functools.partial(update_kernel, chunk),
@@ -325,7 +331,7 @@
         ),
         in_specs=[
             pl.BlockSpec((rows, tile), lambda i: (0, i)),
-            pl.BlockSpec((8, rows), lambda i: (0, 0)),
+            pl.BlockSpec((4, rows), lambda i: (0, 0)),
             pl.BlockSpec((rows, columns), lambda i: (0, 0), **once),
             pl.BlockSpec((tile, columns), lambda i: (i, 0)),
             pl.BlockSpec((tile, columns), lambda i: (i, 0)),
@@ -342,9 +348,11 @@
     own = batches * own_rows
     count = own * parts
     gain_wide = norm_gain.astype(jnp.float32)
-    wide = hidden.reshape(own, features).astype(jnp.float32)
-    factor = lax.rsqrt(jnp.mean(wide * wide, axis=-1, keepdims=True) + EPS)
-    scaled = (wide * factor * gain_wide).astype(jnp.bfloat16)
+    scaled = pl.pallas_call(
+        normalize_kernel,
+        out_shape=jax.ShapeDtypeStruct((own, features), jnp.bfloat16),
+        name="normalize",
+    )(hidden.reshape(own, features), norm_gain.reshape(1, features))
     mine = lax.iota(jnp.int32, parts)[:, None] == lax.axis_index("fsdp")
     label_row = jnp.where(mine, labels.reshape(1, own).astype(jnp.float32), 0.0).reshape(1, count)
 

time: 138 us -> 131 us (0.949)
  Pallas kernels: 130 us -> 125 us
  other arithmetic: 6.46 us -> 2.1 us
    pallas_call x1, Pallas kernels: 44 us -> 39.3 us  [head_update(): pl.pallas_call(functools.partial(update_kernel, chunk), grid=(features //...]
    convert_element_type x2 -> x0, other arithmetic: 2.97 us -> none  [the longest x1 2.27 us: on_device(): scaled = (wide * factor * gain_wide).astype(jnp.bfloat16)]
    pallas_call x0 -> x1, Pallas kernels: none -> 2.46 us  [on_device(): pl.pallas_call(normalize_kernel, out_shape=jax.ShapeDtypeStruct((own, fea...]
    pallas_call x2, Pallas kernels: 24.8 us -> 22.7 us  [exchange(): pl.pallas_call(functools.partial(exchange_kernel, parts, ways, combine),...]
where the time goes in v2:
time: 131 us; the launch traced here: 130 us
  Pallas kernels  125 us (95%)
  other arithmetic  2.1 us (2%)
  local copies, waits for them, and re-layouts  2.08 us (2%)
    pallas_call x1, Pallas kernels, gather_rows(): pl.pallas_call(functools.partial(gather_kernel, parts, ways), out_shape=j...  41.2 us
    pallas_call x1, Pallas kernels, head_update(): pl.pallas_call(functools.partial(update_kernel, chunk), grid=(features //...  39.3 us
    pallas_call x2, Pallas kernels, exchange(): pl.pallas_call(functools.partial(exchange_kernel, parts, ways, combine),...  22.7 us
    pallas_call x1, Pallas kernels, local_logits(): pl.pallas_call(logits_kernel, grid=(columns // tile,), out_shape=(jax.Sha...  19.6 us

profile of v2, /device:TPU:0, one launch (start us, length us, event | category | flops | bytes accessed | tf_op | source)
XLA Modules:
  0.0 130.2 jit_solution(9336433096769030307)
XLA Ops:
  0.6 0.7 convert_element_type.14
  1.3 0.1 convert_element_type.15
  1.4 0.1 broadcast_select_fusion
  1.5 0.7 select_n.15.label_ref
  2.2 1.3 %reshape.55.gain_ref = bf16[1,4096]{1,0:T(2,128)(2,1)} reshape(bf16[4096]{0:T(1024)(128)(2,1)} %param.7) | data formatting | bytes 16384 | tf_op jit(solution)/shard_map/reshape | solution.py:355
  3.5 2.5 %normalize.1.own_ref = bf16[96,4096]{1,0:T(8,128)(2,1)} custom-call(bf16[96,4096]{1,0:T(8,128)(2,1)} %bitcast.5, bf16[1,4096]{1,0:T(2,128)(2,1)} %reshape.55.gain_ref), custom_call_target="tpu_custom_call" | custom-call | tf_op jit(solution)/shard_map/normalize/pallas_call | solution.py:351
  5.9 41.2 %gather_rows.1 = bf16[8,96,4096]{2,1,0:T(8,128)(2,1)} custom-call(bf16[96,4096]{1,0:T(8,128)(2,1)} %normalize.1.own_ref), custom_call_target="tpu_custom_call" | custom-call | tf_op jit(solution)/shard_map/gather_rows/pallas_call | solution.py:130
  47.2 19.6 %local_logits.1 = (f32[768,2048]{1,0:T(8,128)}, f32[4,768]{1,0:T(4,128)}) custom-call(bf16[768,4096]{1,0:T(8,128)(2,1)} %bitcast.3, bf16[4096,2048]{1,0:T(8,128)(2,1)} %weight_ref.3, f32[1,768]{1,0:T(1,128)} %select_n.15.label_ref), custom_call_target="tpu_custom_call" | custom-call | tf_op jit(solution)/shard_map/local_logits/pallas_call | solution.py:264
  66.8 10.7 %exchange_stats.1.stats_ref = f32[4,768]{1,0:T(4,128)} custom-call(f32[4,768]{1,0:T(4,128)} %get-tuple-element.6.x_ref), custom_call_target="tpu_custom_call" | custom-call | tf_op jit(solution)/shard_map/exchange_stats/pallas_call | solution.py:206
  77.4 0.0 copy-start
  77.5 0.0 copy-start.1
  77.5 39.3 %head_update.1 = (f32[4096,2048]{1,0:T(8,128)}, f32[1,4096]{1,0:T(1,128)}) custom-call(bf16[768,4096]{1,0:T(8,128)(2,1)} %bitcast.4, f32[4,768]{1,0:T(4,128)} %exchange_stats.1.stats_ref, f32[768,2048]{1,0:T(8,128)} %get-tuple-element.7.logits_ref, bf16[4096,2048]{1,0:T(8,128)(2,1)} %weight_ref.3, f32[4096,2048]{1,0:T(8,128)} %ema_ref.1), custom_call_target="tpu_custom_call" | custom-call | tf_op jit(solution)/shard_map/head_update/pallas_call | solution.py:325
  116.7 12.1 %exchange_gain.1 = f32[1,4096]{1,0:T(1,128)} custom-call(f32[1,4096]{1,0:T(1,128)} %get-tuple-element.9.x_ref), custom_call_target="tpu_custom_call" | custom-call | tf_op jit(solution)/shard_map/exchange_gain/pallas_call | solution.py:206
  128.8 0.0 copy-done
  128.8 0.0 copy-done.1
  128.8 1.3 %fusion.1 = f32[4096]{0:T(1024)} fusion(f32[4096]{0:T(1024)} %bitcast.6, bf16[4096]{0:T(1024)(128)(2,1)S(1)} %copy-done, f32[4096]{0:T(1024)S(1)} %copy-done.1), kind=kLoop, calls=%fused_computation.2 | loop fusion | flops 28672 | bytes 57344 | tf_op jit(solution)/shard_map/add | solution.py:364
  (1 shorter events, 0.0 us)
Async XLA Ops:
  77.4 51.4 %copy-start = (bf16[4096]{0:T(1024)(128)(2,1)S(1)}, bf16[4096]{0:T(1024)(128)(2,1)}, u32[]{:S(2)}) copy-start(bf16[4096]{0:T(1024)(128)(2,1)} %param.7) | copy-start | bytes 24580
  77.5 51.4 %copy-start.1 = (f32[4096]{0:T(1024)S(1)}, f32[4096]{0:T(1024)}, u32[]{:S(2)}) copy-start(f32[4096]{0:T(1024)} %param.11) | copy-start | bytes 49156
